TPU v7x, 512 devices: a whole 4x8x8 slice. The times are simulated.
512 devices in a mesh: seq: 64 (over y, x, core), head: 8 (over z).
Axes of the slice: x: 4, y: 8, z: 8, core: 2. Of those that a mesh axis runs over, the one named last changes fastest.
Arguments:
- token_values: bfloat16 [24576, 4096], P('seq', 'head'), may hold values from -6 to 6
- b_inputs: bfloat16 [24576, 128], P('seq'), may hold values from -6 to 6
- c_inputs: bfloat16 [24576, 128], P('seq'), may hold values from -6 to 6
- log_decay: float32 [64, 24576], P('head', 'seq'), may hold values from -1 to 0
- grad_out: bfloat16 [24576, 4096], P('seq', 'head'), may hold values from -0.005859375 to 0.005859375
Outputs:
- grad_values: bfloat16 [24576, 4096], P('seq', 'head')
- grad_b: bfloat16 [24576, 128], P('seq')
- grad_c: bfloat16 [24576, 128], P('seq')
All inputs are finite; a program needn't handle non-finite values.
Results may differ from a plain program's by a relative error of at most 0.014.
Values may be sent and summed in bfloat16 or wider, within the bound.
A program may use at most 128 MiB of HBM per device.

v0:
```python
import functools
import jax
import jax.numpy as jnp
from jax import lax
from jax.sharding import PartitionSpec as P

PRECISE = lax.Precision.HIGHEST


def shift(value, count, distance, reverse):
    if reverse:
        pairs = [(p, p - distance) for p in range(distance, count)]
    else:
        pairs = [(p, p + distance) for p in range(count - distance)]
    return lax.ppermute(value, "seq", pairs)


def exclusive_scans(count, decay_cols, parts):
    packed = [jnp.concatenate([decay_cols, s], axis=0) for s, _ in parts]
    windows = [shift(pk, count, 1, rev) for pk, (_, rev) in zip(packed, parts)]
    distance = 1
    while distance < count:
        received = [shift(w, count, distance, rev) for w, (_, rev) in zip(windows, parts)]
        windows = [
            jnp.concatenate([w[:1] * r[:1], w[1:] + w[:1] * r[1:]], axis=0)
            for w, r in zip(windows, received)
        ]
        distance *= 2
    return [w[1:] for w in windows]


def shards(count, token_values, b_inputs, c_inputs, log_decay, grad_out):
    length = token_values.shape[0]
    heads_here = log_decay.shape[0]
    head_dim = token_values.shape[1] // heads_here
    state_size = b_inputs.shape[1]
    cumulative = jnp.cumsum(log_decay, axis=1)
    block_log = cumulative[:, -1]
    into_end = jnp.exp(block_log[:, None] - cumulative)
    from_start = jnp.exp(cumulative)
    block_decay = jnp.exp(block_log)
    b_float = b_inputs.astype(jnp.float32)
    c_float = c_inputs.astype(jnp.float32)
    decayed_b = (into_end[:, :, None] * b_float[None]).astype(jnp.bfloat16)
    decayed_c = (from_start[:, :, None] * c_float[None]).astype(jnp.bfloat16)
    x_heads = token_values.reshape(length, heads_here, head_dim)
    dy_heads = grad_out.reshape(length, heads_here, head_dim)
    state_local = jnp.einsum(
        "htn,thp->nhp", decayed_b, x_heads, preferred_element_type=jnp.float32
    ).reshape(state_size, heads_here * head_dim)
    adjoint_local = jnp.einsum(
        "hsn,shp->nhp", decayed_c, dy_heads, preferred_element_type=jnp.float32
    ).reshape(state_size, heads_here * head_dim)
    decay_cols = jnp.repeat(block_decay, head_dim)[None, :]
    state_in, adjoint_out = exclusive_scans(
        count, decay_cols, [(state_local, False), (adjoint_local, True)]
    )
    scores = lax.dot_general(
        c_inputs, b_inputs, (((1,), (1,)), ((), ())), preferred_element_type=jnp.float32
    )
    entry_indices = lax.iota(jnp.int32, length)
    causal = entry_indices[:, None] >= entry_indices[None, :]

    def head_step(head_idx, carried):
        running, dx_local = carried
        cum_head = lax.dynamic_index_in_dim(cumulative, head_idx, 0, keepdims=False)
        log_gaps = cum_head[:, None] - cum_head[None, :]
        decays = jnp.where(causal, jnp.exp(jnp.where(causal, log_gaps, 0.0)), 0.0)
        mixing = (scores * decays).astype(jnp.bfloat16)
        x_head = lax.dynamic_slice_in_dim(token_values, head_idx * head_dim, head_dim, 1)
        dy_head = lax.dynamic_slice_in_dim(grad_out, head_idx * head_dim, head_dim, 1)
        dx_head = lax.dot_general(
            mixing, dy_head, (((0,), (0,)), ((), ())), preferred_element_type=jnp.float32
        )
        dot_pairs = lax.dot_general(
            dy_head, x_head, (((1,), (1,)), ((), ())), preferred_element_type=jnp.float32
        )
        dx_local = lax.dynamic_update_slice_in_dim(dx_local, dx_head, head_idx * head_dim, 1)
        return (running + decays * dot_pairs, dx_local)

    start_pair = (
        jnp.zeros((length, length), jnp.float32),
        jnp.zeros((length, heads_here * head_dim), jnp.float32),
    )
    running, dx_local = lax.fori_loop(0, heads_here, head_step, start_pair)
    weighted = running.astype(jnp.bfloat16)
    db_part = lax.dot_general(
        weighted, c_inputs, (((0,), (0,)), ((), ())), preferred_element_type=jnp.float32
    )
    dc_part = jnp.dot(weighted, b_inputs, preferred_element_type=jnp.float32)
    to_end_cols = jnp.repeat(into_end.T, head_dim, axis=1)
    from_start_cols = jnp.repeat(from_start.T, head_dim, axis=1)
    grad_values = dx_local + to_end_cols * jnp.dot(b_float, adjoint_out, precision=PRECISE)
    db_part = db_part + jnp.dot(
        token_values.astype(jnp.float32) * to_end_cols, adjoint_out.T, precision=PRECISE
    )
    dc_part = dc_part + jnp.dot(
        grad_out.astype(jnp.float32) * from_start_cols, state_in.T, precision=PRECISE
    )
    grad_b, grad_c = (
        lax.psum(db_part.astype(jnp.bfloat16), "head").astype(jnp.float32),
        lax.psum(dc_part.astype(jnp.bfloat16), "head").astype(jnp.float32),
    )
    return (
        grad_values.astype(jnp.bfloat16),
        grad_b.astype(jnp.bfloat16),
        grad_c.astype(jnp.bfloat16),
    )


def solution(mesh):
    in_specs = (
        P("seq", "head"),
        P("seq", None),
        P("seq", None),
        P("head", "seq"),
        P("seq", "head"),
    )
    out_specs = (P("seq", "head"), P("seq", None), P("seq", None))
    body = functools.partial(shards, mesh.shape["seq"])
    return jax.shard_map(body, mesh=mesh, in_specs=in_specs, out_specs=out_specs, check_vma=False)
```

profile of v0, /device:TPU:2, one launch (start us, length us, event | category | flops | bytes accessed | tf_op | source)
XLA Modules:
  0.0 233.3 jit_solution(7088750057124576250)
XLA Ops:
  7.2 1.9 reduce-window.6
  9.2 0.2 slice_reduce_fusion
  9.4 0.2 slice_reduce_fusion.1
  9.8 1.2 copy.15
  11.1 0.6 fusion.21
  11.9 0.2 copy-done.2
  12.1 0.2 copy.13
  12.3 0.3 copy-done.1
  12.7 0.6 fusion.20
  13.4 0.8 pad_maximum_fusion
  14.2 1.9 collective-permute-start
  16.1 2.4 %collective-permute-start.7 = (f32[129,512]{1,0:T(8,128)S(1)}, f32[129,512]{1,0:T(8,128)}, u32[]{:S(2)}, u32[]{:S(2)}) collective-permute-start(f32[129,512]{1,0:T(8,128)S(1)} %get-tuple-element.224), channel_id=1, source_target_pairs={{0,8},{8,16},{16,24},{24,32},{32,40},{40,48},{48,56},{56,64},{64,7... | collective-permute-start | bytes 792584 | tf_op jit(solution)/shard_map/ppermute | solution.py:15
  18.6 0.3 fusion.47
  18.9 21.5 %while.17 = (s32[]{:T(128)}, f32[384,384]{1,0:T(8,128)S(1)}, f32[384,512]{0,1:T(8,128)S(1)}, f32[8,384]{1,0:T(8,128)S(1)}, bf16[384,512]{1,0:T(8,128)(2,1)}, /*i...) while((s32[]{:T(128)}, f32[384,384]{1,0:T(8,128)S(1)}, ...), condition=%wide.region_3.4_spmd.clone.clone, body=%wide.region_2.3_spmd.clone.clone.sunk | while | flops 39665672 | bytes 2176688 | solution.py:85
  18.9 1.4 fusion.64
  20.3 1.2 convolution_dynamic-update-slice_fusion.2
  21.6 1.4 fusion.64
  23.0 1.2 convolution_dynamic-update-slice_fusion.2
  24.3 1.4 fusion.64
  25.7 1.2 convolution_dynamic-update-slice_fusion.2
  27.0 1.4 fusion.64
  28.4 1.2 convolution_dynamic-update-slice_fusion.2
  29.7 1.4 fusion.64
  31.1 1.2 convolution_dynamic-update-slice_fusion.2
  32.3 1.4 fusion.64
  33.7 1.2 convolution_dynamic-update-slice_fusion.2
  35.0 1.4 fusion.64
  36.4 1.2 convolution_dynamic-update-slice_fusion.2
  37.7 1.4 fusion.64
  39.1 1.2 convolution_dynamic-update-slice_fusion.2
  40.4 7.4 %collective-permute-start.1 = (f32[129,512]{1,0:T(8,128)}, f32[129,512]{1,0:T(8,128)S(1)}, u32[]{:S(2)}, u32[]{:S(2)}) collective-permute-start(f32[129,512]{1,0:T(8,128)} %collective-permute-done), channel_id=1, source_target_pairs={{8,0},{16,8},{24,16},{32,24},{40,32},{48,40},{56,48},{64,56},{72,6... | collective-permute-start | bytes 792584 | tf_op jit(solution)/shard_map/ppermute | solution.py:15
  47.8 0.3 fusion.41
  48.2 0.2 fusion.39
  48.5 1.9 collective-permute-start.8
  50.4 1.8 collective-permute-done.1
  52.2 0.7 slice_multiply_fusion.21
  52.9 1.0 fusion.38
  53.9 1.9 collective-permute-start.2
  55.9 0.7 collective-permute-done.8
  56.5 0.7 slice_multiply_fusion.16
  57.3 1.0 fusion.32
  58.3 3.3 %collective-permute-start.9 = (f32[129,512]{1,0:T(8,128)S(1)}, f32[129,512]{1,0:T(8,128)S(1)}, u32[]{:S(2)}, u32[]{:S(2)}) collective-permute-start(f32[129,512]{1,0:T(8,128)S(1)} %pad_maximum_fusion.7), channel_id=1, source_target_pairs={{0,16},{8,24},{16,32},{24,40},{32,48},{40,56},{48,64},{56,72},{64,... | collective-permute-start | bytes 792584 | tf_op jit(solution)/shard_map/ppermute | solution.py:15
  61.6 0.8 collective-permute-done.2
  62.5 1.3 collective-permute-start.3
  63.8 11.6 %collective-permute-done.9 = f32[129,512]{1,0:T(8,128)S(1)} collective-permute-done((f32[129,512]{1,0:T(8,128)S(1)}, f32[129,512]{1,0:T(8,128)S(1)}, u32[]{:S(2)}, u32[]{:S(2)}) %collective-permute-start.9) | collective-permute-done | bytes 264224 | tf_op jit(solution)/shard_map/ppermute | solution.py:15
  75.5 2.3 collective-permute-start.10
  78.0 1.3 collective-permute-start.4
  79.3 5.3 %collective-permute-done.10 = f32[129,512]{1,0:T(8,128)S(1)} collective-permute-done((f32[129,512]{1,0:T(8,128)S(1)}, f32[129,512]{1,0:T(8,128)S(1)}, u32[]{:S(2)}, u32[]{:S(2)}) %collective-permute-start.10) | collective-permute-done | bytes 264224 | tf_op jit(solution)/shard_map/ppermute | solution.py:15
  84.7 7.9 %collective-permute-start.11 = (f32[129,512]{1,0:T(8,128)S(1)}, f32[129,512]{1,0:T(8,128)S(1)}, u32[]{:S(2)}, u32[]{:S(2)}) collective-permute-start(f32[129,512]{1,0:T(8,128)S(1)} %pad_maximum_fusion.9), channel_id=1, source_target_pairs={{0,64},{8,72},{16,80},{24,88},{32,96},{40,104},{48,112},{56,120},{... | collective-permute-start | bytes 792584 | tf_op jit(solution)/shard_map/ppermute | solution.py:15
  92.7 1.3 collective-permute-start.5
  94.0 4.1 %collective-permute-done.11 = f32[129,512]{1,0:T(8,128)S(1)} collective-permute-done((f32[129,512]{1,0:T(8,128)S(1)}, f32[129,512]{1,0:T(8,128)S(1)}, u32[]{:S(2)}, u32[]{:S(2)}) %collective-permute-start.11) | collective-permute-done | bytes 264224 | tf_op jit(solution)/shard_map/ppermute | solution.py:15
  98.3 5.4 %collective-permute-start.12 = (f32[129,512]{1,0:T(8,128)S(1)}, f32[129,512]{1,0:T(8,128)S(1)}, u32[]{:S(2)}, u32[]{:S(2)}) collective-permute-start(f32[129,512]{1,0:T(8,128)S(1)} %pad_maximum_fusion.10), channel_id=1, source_target_pairs={{0,128},{8,136},{16,144},{24,152},{32,160},{40,168},{48,176},{56,1... | collective-permute-start | bytes 792584 | tf_op jit(solution)/shard_map/ppermute | solution.py:15
  103.7 5.6 %collective-permute-done.5 = f32[129,512]{1,0:T(8,128)S(1)} collective-permute-done((f32[129,512]{1,0:T(8,128)S(1)}, f32[129,512]{1,0:T(8,128)S(1)}, u32[]{:S(2)}, u32[]{:S(2)}) %collective-permute-start.5) | collective-permute-done | bytes 264224 | tf_op jit(solution)/shard_map/ppermute | solution.py:15
  109.4 1.3 collective-permute-start.6
  110.8 17.8 %collective-permute-start.13 = (f32[129,512]{1,0:T(8,128)S(1)}, f32[129,512]{1,0:T(8,128)S(1)}, u32[]{:S(2)}, u32[]{:S(2)}) collective-permute-start(f32[129,512]{1,0:T(8,128)S(1)} %pad_maximum_fusion.11), channel_id=1, source_target_pairs={{0,256},{8,264},{16,272},{24,280},{32,288},{40,296},{48,304},{56,3... | collective-permute-start | bytes 792584 | tf_op jit(solution)/shard_map/ppermute | solution.py:15
  128.7 0.5 collective-permute-done.6
  129.2 2.1 fusion.18
  131.3 3.5 %collective-permute-done.13 = f32[129,512]{1,0:T(8,128)S(1)} collective-permute-done((f32[129,512]{1,0:T(8,128)S(1)}, f32[129,512]{1,0:T(8,128)S(1)}, u32[]{:S(2)}, u32[]{:S(2)}) %collective-permute-start.13) | collective-permute-done | bytes 264224 | tf_op jit(solution)/shard_map/ppermute | solution.py:15
  134.7 2.1 fusion.19
  136.9 0.7 fusion.17
  137.6 0.9 copy.19
  138.5 84.9 %all-reduce.3.cloned.1.call-done = (bf16[384,128]{1,0:T(8,128)(2,1)}, bf16[384,128]{1,0:T(8,128)(2,1)}) async-done(((bf16[384,128]{1,0:T(8,128)(2,1)}, bf16[384,128]{1,0:T(8,128)(2,1)}), (bf16[384,128]{1,0:T(8,128)(2,1)}, bf16[384,128]{1,0:T(8,128)(2,1)})) %all-reduce.3.cloned.1.call-update) | async-done | bytes 196624 | tf_op jit(solution)/shard_map/psum | solution.py:101
  223.4 1.5 copy.32
  224.9 1.5 copy.33
  (60 shorter events, 1.8 us)
Async XLA Ops:
  7.2 3.9 %copy-start = (bf16[384,128]{1,0:T(8,128)(2,1)S(1)}, bf16[384,128]{1,0:T(8,128)(2,1)}, u32[]{:S(2)}) copy-start(bf16[384,128]{1,0:T(8,128)(2,1)} %param.8) | copy-start | bytes 294916
  7.2 216.2 %all-reduce.3.cloned.1.call-start = ((), (), s32[]{:S(2)}) async-start(), calls=%async_computation | async-start | bytes 393216 | tf_op jit(solution)/shard_map/psum | solution.py:101
  11.1 1.0 copy-start.2
  11.7 0.9 copy-start.1
  14.2 26.1 %collective-permute-start = (f32[129,512]{1,0:T(8,128)}, f32[129,512]{1,0:T(8,128)}, u32[]{:S(2)}, u32[]{:S(2)}) collective-permute-start(f32[129,512]{1,0:T(8,128)} %get-tuple-element.225), channel_id=1, source_target_pairs={{8,0},{16,8},{24,16},{32,24},{40,32},{48,40},{56,48},{64,56},{72,6... | collective-permute-start | bytes 792584 | tf_op jit(solution)/shard_map/ppermute | solution.py:15
  16.1 32.3 %collective-permute-start.7 = (f32[129,512]{1,0:T(8,128)S(1)}, f32[129,512]{1,0:T(8,128)}, u32[]{:S(2)}, u32[]{:S(2)}) collective-permute-start(f32[129,512]{1,0:T(8,128)S(1)} %get-tuple-element.224), channel_id=1, source_target_pairs={{0,8},{8,16},{16,24},{24,32},{32,40},{40,48},{48,56},{56,64},{64,7... | collective-permute-start | bytes 792584 | tf_op jit(solution)/shard_map/ppermute | solution.py:15
  40.4 11.8 %collective-permute-start.1 = (f32[129,512]{1,0:T(8,128)}, f32[129,512]{1,0:T(8,128)S(1)}, u32[]{:S(2)}, u32[]{:S(2)}) collective-permute-start(f32[129,512]{1,0:T(8,128)} %collective-permute-done), channel_id=1, source_target_pairs={{8,0},{16,8},{24,16},{32,24},{40,32},{48,40},{56,48},{64,56},{72,6... | collective-permute-start | bytes 792584 | tf_op jit(solution)/shard_map/ppermute | solution.py:15
  48.5 8.1 %collective-permute-start.8 = (f32[129,512]{1,0:T(8,128)}, f32[129,512]{1,0:T(8,128)S(1)}, u32[]{:S(2)}, u32[]{:S(2)}) collective-permute-start(f32[129,512]{1,0:T(8,128)} %collective-permute-done.7), channel_id=1, source_target_pairs={{0,8},{8,16},{16,24},{24,32},{32,40},{40,48},{48,56},{56,64},{64,7... | collective-permute-start | bytes 792584 | tf_op jit(solution)/shard_map/ppermute | solution.py:15
  53.9 8.4 %collective-permute-start.2 = (f32[129,512]{1,0:T(8,128)S(1)}, f32[129,512]{1,0:T(8,128)S(1)}, u32[]{:S(2)}, u32[]{:S(2)}) collective-permute-start(f32[129,512]{1,0:T(8,128)S(1)} %pad_maximum_fusion.2), channel_id=1, source_target_pairs={{16,0},{24,8},{32,16},{40,24},{48,32},{56,40},{64,48},{72,56},{80,... | collective-permute-start | bytes 792584 | tf_op jit(solution)/shard_map/ppermute | solution.py:15
  58.3 17.1 %collective-permute-start.9 = (f32[129,512]{1,0:T(8,128)S(1)}, f32[129,512]{1,0:T(8,128)S(1)}, u32[]{:S(2)}, u32[]{:S(2)}) collective-permute-start(f32[129,512]{1,0:T(8,128)S(1)} %pad_maximum_fusion.7), channel_id=1, source_target_pairs={{0,16},{8,24},{16,32},{24,40},{32,48},{40,56},{48,64},{56,72},{64,... | collective-permute-start | bytes 792584 | tf_op jit(solution)/shard_map/ppermute | solution.py:15
  62.5 15.4 %collective-permute-start.3 = (f32[129,512]{1,0:T(8,128)S(1)}, f32[129,512]{1,0:T(8,128)S(1)}, u32[]{:S(2)}, u32[]{:S(2)}) collective-permute-start(f32[129,512]{1,0:T(8,128)S(1)} %pad_maximum_fusion.3), channel_id=1, source_target_pairs={{32,0},{40,8},{48,16},{56,24},{64,32},{72,40},{80,48},{88,56},{96,... | collective-permute-start | bytes 792584 | tf_op jit(solution)/shard_map/ppermute | solution.py:15
  75.5 9.1 %collective-permute-start.10 = (f32[129,512]{1,0:T(8,128)S(1)}, f32[129,512]{1,0:T(8,128)S(1)}, u32[]{:S(2)}, u32[]{:S(2)}) collective-permute-start(f32[129,512]{1,0:T(8,128)S(1)} %pad_maximum_fusion.8), channel_id=1, source_target_pairs={{0,32},{8,40},{16,48},{24,56},{32,64},{40,72},{48,80},{56,88},{64,... | collective-permute-start | bytes 792584 | tf_op jit(solution)/shard_map/ppermute | solution.py:15
  78.0 14.7 %collective-permute-start.4 = (f32[129,512]{1,0:T(8,128)S(1)}, f32[129,512]{1,0:T(8,128)S(1)}, u32[]{:S(2)}, u32[]{:S(2)}) collective-permute-start(f32[129,512]{1,0:T(8,128)S(1)} %pad_maximum_fusion.4), channel_id=1, source_target_pairs={{64,0},{72,8},{80,16},{88,24},{96,32},{104,40},{112,48},{120,56},{... | collective-permute-start | bytes 792584 | tf_op jit(solution)/shard_map/ppermute | solution.py:15
  84.7 13.5 %collective-permute-start.11 = (f32[129,512]{1,0:T(8,128)S(1)}, f32[129,512]{1,0:T(8,128)S(1)}, u32[]{:S(2)}, u32[]{:S(2)}) collective-permute-start(f32[129,512]{1,0:T(8,128)S(1)} %pad_maximum_fusion.9), channel_id=1, source_target_pairs={{0,64},{8,72},{16,80},{24,88},{32,96},{40,104},{48,112},{56,120},{... | collective-permute-start | bytes 792584 | tf_op jit(solution)/shard_map/ppermute | solution.py:15
  92.7 16.6 %collective-permute-start.5 = (f32[129,512]{1,0:T(8,128)S(1)}, f32[129,512]{1,0:T(8,128)S(1)}, u32[]{:S(2)}, u32[]{:S(2)}) collective-permute-start(f32[129,512]{1,0:T(8,128)S(1)} %pad_maximum_fusion.5), channel_id=1, source_target_pairs={{128,0},{136,8},{144,16},{152,24},{160,32},{168,40},{176,48},{184,... | collective-permute-start | bytes 792584 | tf_op jit(solution)/shard_map/ppermute | solution.py:15
  98.3 12.5 %collective-permute-start.12 = (f32[129,512]{1,0:T(8,128)S(1)}, f32[129,512]{1,0:T(8,128)S(1)}, u32[]{:S(2)}, u32[]{:S(2)}) collective-permute-start(f32[129,512]{1,0:T(8,128)S(1)} %pad_maximum_fusion.10), channel_id=1, source_target_pairs={{0,128},{8,136},{16,144},{24,152},{32,160},{40,168},{48,176},{56,1... | collective-permute-start | bytes 792584 | tf_op jit(solution)/shard_map/ppermute | solution.py:15
  109.4 19.8 %collective-permute-start.6 = (f32[129,512]{1,0:T(8,128)S(1)}, f32[129,512]{1,0:T(8,128)S(1)}, u32[]{:S(2)}, u32[]{:S(2)}) collective-permute-start(f32[129,512]{1,0:T(8,128)S(1)} %pad_maximum_fusion.6), channel_id=1, source_target_pairs={{256,0},{264,8},{272,16},{280,24},{288,32},{296,40},{304,48},{312,... | collective-permute-start | bytes 792584 | tf_op jit(solution)/shard_map/ppermute | solution.py:15
  110.8 23.9 %collective-permute-start.13 = (f32[129,512]{1,0:T(8,128)S(1)}, f32[129,512]{1,0:T(8,128)S(1)}, u32[]{:S(2)}, u32[]{:S(2)}) collective-permute-start(f32[129,512]{1,0:T(8,128)S(1)} %pad_maximum_fusion.11), channel_id=1, source_target_pairs={{0,256},{8,264},{16,272},{24,280},{32,288},{40,296},{48,304},{56,3... | collective-permute-start | bytes 792584 | tf_op jit(solution)/shard_map/ppermute | solution.py:15
Sparse Core Ops, SparseCore 0:
  136.9 86.3 all-reduce.2
where the time goes:
time: 235 us; the launch traced here: 233 us
  waiting for transfers between devices  119 us (51%)
  starting transfers between devices  57.6 us (25%)
  matrix products  27.7 us (12%)
  between operations  14.5 us (6%)
  other arithmetic  7.18 us (3%)
  local copies, waits for them, and re-layouts  7.07 us (3%)
    psum x1, waiting for transfers between devices, shards(): lax.psum(db_part.astype(jnp.bfloat16), 'head').astype(jnp.float32)  84.9 us
    ppermute x14, starting transfers between devices, shift(): return lax.ppermute(value, 'seq', pairs)  57.5 us
    ppermute x14, waiting for transfers between devices, shift(): return lax.ppermute(value, 'seq', pairs)  34 us
    dot_general x8, matrix products, head_step(): lax.dot_general(dy_head, x_head, (((1,), (1,)), ((), ())), preferred_elem...  11.2 us
    dot_general x8, matrix products, head_step(): lax.dot_general(mixing, dy_head, (((0,), (0,)), ((), ())), preferred_elem...  9.8 us
    unnamed x11, local copies, waits for them, and re-layouts  6.02 us
  transfers between devices with their start and end apart: 15, of which 10 were waited for; matrix products, arithmetic and copies ran while one was open for 13% of the time, Pallas kernels for 0%

commit v1 on v0

--- a/solution.py
+++ b/solution.py
@@ -5,6 +5,11 @@
 from jax.sharding import PartitionSpec as P
 
 PRECISE = lax.Precision.HIGHEST
+
+
+def finish_tiles_over_axis(matrix, lane_axis):
+    w1 = lax.all_gather(matrix, axis_name=lane_axis)
+    return jnp.sum(w1, axis=0)
 
 
 def shift(value, count, distance, reverse):
@@ -98,7 +103,7 @@
         grad_out.astype(jnp.float32) * from_start_cols, state_in.T, precision=PRECISE
     )
     grad_b, grad_c = (
-        lax.psum(db_part.astype(jnp.bfloat16), "head").astype(jnp.float32),
+        finish_tiles_over_axis(db_part.astype(jnp.bfloat16), "head").astype(jnp.float32),
         lax.psum(dc_part.astype(jnp.bfloat16), "head").astype(jnp.float32),
     )
     return (

time: 235 us -> 245 us (1.043)
  blocking collectives: 0 us -> 32.7 us
  waiting for transfers between devices: 119 us -> 105 us
  matrix products: 27.7 us -> 19.6 us
    all_gather x0 -> x1, blocking collectives: none -> 32.7 us  [finish_tiles_over_axis(): w1 = lax.all_gather(matrix, axis_name=lane_axis)]
    psum x1, waiting for transfers between devices: 84.9 us -> 74.9 us  [shards(): lax.psum(dc_part.astype(jnp.bfloat16), 'head').astype(jnp.float32)]
    dot_general x8, matrix products: 9.8 us -> 2.7 us  [head_step(): lax.dot_general(mixing, dy_head, (((0,), (0,)), ((), ())), preferred_elem...]
    ppermute x14, waiting for transfers between devices: 34 us -> 30.5 us  [shift(): return lax.ppermute(value, 'seq', pairs)]
    unnamed x11 -> x10, local copies, waits for them, and re-layouts: 6.02 us -> 4.49 us
  transfers between devices with their start and end apart: 15 -> 15, of which waited for: 10 -> 9; matrix products, arithmetic and copies ran while one was open for 13% -> 9% of each run, Pallas kernels for 0% -> 0%
where the time goes in v1:
time: 245 us; the launch traced here: 244 us
  waiting for transfers between devices  105 us (43%)
  starting transfers between devices  57.6 us (24%)
  blocking collectives  32.7 us (13%)
  matrix products  19.6 us (8%)
  between operations  14.5 us (6%)
  other arithmetic  8.02 us (3%)
  local copies, waits for them, and re-layouts  5.53 us (2%)
    psum x1, waiting for transfers between devices, shards(): lax.psum(dc_part.astype(jnp.bfloat16), 'head').astype(jnp.float32)  74.9 us
    ppermute x14, starting transfers between devices, shift(): return lax.ppermute(value, 'seq', pairs)  57.5 us
    all_gather x1, blocking collectives, finish_tiles_over_axis(): w1 = lax.all_gather(matrix, axis_name=lane_axis)  32.7 us
    ppermute x14, waiting for transfers between devices, shift(): return lax.ppermute(value, 'seq', pairs)  30.5 us
    dot_general x8, matrix products, head_step(): lax.dot_general(dy_head, x_head, (((1,), (1,)), ((), ())), preferred_elem...  10.8 us
  transfers between devices with their start and end apart: 15, of which 9 were waited for; matrix products, arithmetic and copies ran while one was open for 9% of the time, Pallas kernels for 0%

profile of v1, /device:TPU:2, one launch (start us, length us, event | category | flops | bytes accessed | tf_op | source)
XLA Modules:
  0.0 243.7 jit_solution(2287746485624188373)
XLA Ops:
  7.2 1.9 reduce-window.6
  9.2 0.2 slice_reduce_fusion
  9.4 0.2 slice_reduce_fusion.1
  9.8 1.2 copy.15
  11.1 0.6 fusion.21
  11.9 0.2 copy-done.2
  12.1 0.2 copy.13
  12.3 0.3 copy-done.1
  12.7 0.6 fusion.20
  13.5 0.9 pad_maximum_fusion
  14.3 1.9 collective-permute-start
  16.2 2.4 collective-permute-start.7
  18.7 0.3 fusion.47
  19.0 14.0 %while.17 = (s32[]{:T(128)}, f32[384,384]{1,0:T(8,128)S(1)}, f32[384,512]{0,1:T(8,128)S(1)}, f32[8,384]{1,0:T(8,128)S(1)}, bf16[384,512]{1,0:T(8,128)(2,1)S(1)},...) while((s32[]{:T(128)}, f32[384,384]{1,0:T(8,128)S(1)}, ...), condition=%wide.region_3.4_spmd.clone.clone, body=%wide.region_2.3_spmd.clone.clone.sunk | while | flops 39665672 | bytes 2176688 | solution.py:90
  19.0 1.3 fusion.64
  20.4 0.3 convolution_dynamic-update-slice_fusion.2
  20.8 1.3 fusion.64
  22.1 0.3 convolution_dynamic-update-slice_fusion.2
  22.5 1.3 fusion.64
  23.9 0.3 convolution_dynamic-update-slice_fusion.2
  24.3 1.3 fusion.64
  25.6 0.3 convolution_dynamic-update-slice_fusion.2
  26.0 1.3 fusion.64
  27.4 0.3 convolution_dynamic-update-slice_fusion.2
  27.8 1.3 fusion.64
  29.1 0.3 convolution_dynamic-update-slice_fusion.2
  29.5 1.3 fusion.64
  30.9 0.3 convolution_dynamic-update-slice_fusion.2
  31.2 1.3 fusion.64
  32.6 0.3 convolution_dynamic-update-slice_fusion.2
  33.0 7.4 %collective-permute-start.1 = (f32[129,512]{1,0:T(8,128)}, f32[129,512]{1,0:T(8,128)S(1)}, u32[]{:S(2)}, u32[]{:S(2)}) collective-permute-start(f32[129,512]{1,0:T(8,128)} %collective-permute-done), channel_id=1, source_target_pairs={{8,0},{16,8},{24,16},{32,24},{40,32},{48,40},{56,48},{64,56},{72,6... | collective-permute-start | bytes 792584 | tf_op jit(solution)/shard_map/ppermute | solution.py:20
  40.4 0.3 fusion.41
  40.8 0.2 fusion.39
  41.1 1.9 collective-permute-start.8
  43.0 1.8 collective-permute-done.1
  44.8 0.7 slice_multiply_fusion.21
  45.5 1.0 fusion.38
  46.5 1.9 collective-permute-start.2
  48.5 0.7 collective-permute-done.8
  49.2 0.7 slice_multiply_fusion.16
  49.9 1.0 fusion.32
  50.9 3.2 %collective-permute-start.9 = (f32[129,512]{1,0:T(8,128)S(1)}, f32[129,512]{1,0:T(8,128)S(1)}, u32[]{:S(2)}, u32[]{:S(2)}) collective-permute-start(f32[129,512]{1,0:T(8,128)S(1)} %pad_maximum_fusion.7), channel_id=1, source_target_pairs={{0,16},{8,24},{16,32},{24,40},{32,48},{40,56},{48,64},{56,72},{64,... | collective-permute-start | bytes 792584 | tf_op jit(solution)/shard_map/ppermute | solution.py:20
  54.2 0.8 collective-permute-done.2
  55.1 1.3 collective-permute-start.3
  56.4 11.7 %collective-permute-done.9 = f32[129,512]{1,0:T(8,128)S(1)} collective-permute-done((f32[129,512]{1,0:T(8,128)S(1)}, f32[129,512]{1,0:T(8,128)S(1)}, u32[]{:S(2)}, u32[]{:S(2)}) %collective-permute-start.9) | collective-permute-done | bytes 264224 | tf_op jit(solution)/shard_map/ppermute | solution.py:20
  68.2 2.3 collective-permute-start.10
  70.6 1.3 collective-permute-start.4
  71.9 5.3 %collective-permute-done.10 = f32[129,512]{1,0:T(8,128)S(1)} collective-permute-done((f32[129,512]{1,0:T(8,128)S(1)}, f32[129,512]{1,0:T(8,128)S(1)}, u32[]{:S(2)}, u32[]{:S(2)}) %collective-permute-start.10) | collective-permute-done | bytes 264224 | tf_op jit(solution)/shard_map/ppermute | solution.py:20
  77.3 7.9 %collective-permute-start.11 = (f32[129,512]{1,0:T(8,128)S(1)}, f32[129,512]{1,0:T(8,128)S(1)}, u32[]{:S(2)}, u32[]{:S(2)}) collective-permute-start(f32[129,512]{1,0:T(8,128)S(1)} %pad_maximum_fusion.9), channel_id=1, source_target_pairs={{0,64},{8,72},{16,80},{24,88},{32,96},{40,104},{48,112},{56,120},{... | collective-permute-start | bytes 792584 | tf_op jit(solution)/shard_map/ppermute | solution.py:20
  85.3 1.3 collective-permute-start.5
  86.6 4.1 %collective-permute-done.11 = f32[129,512]{1,0:T(8,128)S(1)} collective-permute-done((f32[129,512]{1,0:T(8,128)S(1)}, f32[129,512]{1,0:T(8,128)S(1)}, u32[]{:S(2)}, u32[]{:S(2)}) %collective-permute-start.11) | collective-permute-done | bytes 264224 | tf_op jit(solution)/shard_map/ppermute | solution.py:20
  90.9 5.4 %collective-permute-start.12 = (f32[129,512]{1,0:T(8,128)S(1)}, f32[129,512]{1,0:T(8,128)S(1)}, u32[]{:S(2)}, u32[]{:S(2)}) collective-permute-start(f32[129,512]{1,0:T(8,128)S(1)} %pad_maximum_fusion.10), channel_id=1, source_target_pairs={{0,128},{8,136},{16,144},{24,152},{32,160},{40,168},{48,176},{56,1... | collective-permute-start | bytes 792584 | tf_op jit(solution)/shard_map/ppermute | solution.py:20
  96.3 5.6 %collective-permute-done.5 = f32[129,512]{1,0:T(8,128)S(1)} collective-permute-done((f32[129,512]{1,0:T(8,128)S(1)}, f32[129,512]{1,0:T(8,128)S(1)}, u32[]{:S(2)}, u32[]{:S(2)}) %collective-permute-start.5) | collective-permute-done | bytes 264224 | tf_op jit(solution)/shard_map/ppermute | solution.py:20
  102.0 1.3 collective-permute-start.6
  103.4 17.8 %collective-permute-start.13 = (f32[129,512]{1,0:T(8,128)S(1)}, f32[129,512]{1,0:T(8,128)S(1)}, u32[]{:S(2)}, u32[]{:S(2)}) collective-permute-start(f32[129,512]{1,0:T(8,128)S(1)} %pad_maximum_fusion.11), channel_id=1, source_target_pairs={{0,256},{8,264},{16,272},{24,280},{32,288},{40,296},{48,304},{56,3... | collective-permute-start | bytes 792584 | tf_op jit(solution)/shard_map/ppermute | solution.py:20
  121.3 0.6 collective-permute-done.6
  121.8 1.4 fusion.18
  123.2 32.7 %all-gather = bf16[3072,128]{1,0:T(8,128)(2,1)S(1)} all-gather(bf16[384,128]{1,0:T(8,128)(2,1)S(1)} %fusion.18), channel_id=2, replica_groups=mesh['seq'=64,'head'=8] {'head'}, dimensions={0}, use_global_device_ids=true | all-gather | bytes 884736 | tf_op jit(solution)/shard_map/all_gather | solution.py:11
  155.9 2.0 fusion.19
  158.0 0.7 fusion.17
  158.7 0.9 copy.19
  159.7 0.8 reduce_sum.12
  160.4 74.9 %all-reduce.2.cloned.1.call-done = bf16[384,128]{1,0:T(8,128)(2,1)} async-done(((bf16[384,128]{1,0:T(8,128)(2,1)}), bf16[384,128]{1,0:T(8,128)(2,1)}) %all-reduce.2.cloned.1.call-update) | async-done | bytes 98320 | tf_op jit(solution)/shard_map/psum | solution.py:107
  235.3 1.5 copy.31
  (61 shorter events, 1.8 us)
Async XLA Ops:
  7.2 3.9 %copy-start = (bf16[384,128]{1,0:T(8,128)(2,1)S(1)}, bf16[384,128]{1,0:T(8,128)(2,1)}, u32[]{:S(2)}) copy-start(bf16[384,128]{1,0:T(8,128)(2,1)} %param.8) | copy-start | bytes 294916
  7.2 228.1 %all-reduce.2.cloned.1.call-start = ((), (), s32[]{:S(2)}) async-start(), calls=%async_computation | async-start | bytes 196608 | tf_op jit(solution)/shard_map/psum | solution.py:107
  11.1 1.0 copy-start.2
  11.8 0.9 copy-start.1
  14.3 18.6 %collective-permute-start = (f32[129,512]{1,0:T(8,128)}, f32[129,512]{1,0:T(8,128)}, u32[]{:S(2)}, u32[]{:S(2)}) collective-permute-start(f32[129,512]{1,0:T(8,128)} %get-tuple-element.223), channel_id=1, source_target_pairs={{8,0},{16,8},{24,16},{32,24},{40,32},{48,40},{56,48},{64,56},{72,6... | collective-permute-start | bytes 792584 | tf_op jit(solution)/shard_map/ppermute | solution.py:20
  16.2 24.8 %collective-permute-start.7 = (f32[129,512]{1,0:T(8,128)}, f32[129,512]{1,0:T(8,128)}, u32[]{:S(2)}, u32[]{:S(2)}) collective-permute-start(f32[129,512]{1,0:T(8,128)} %get-tuple-element.222), channel_id=1, source_target_pairs={{0,8},{8,16},{16,24},{24,32},{32,40},{40,48},{48,56},{56,64},{64,7... | collective-permute-start | bytes 792584 | tf_op jit(solution)/shard_map/ppermute | solution.py:20
  33.0 11.8 %collective-permute-start.1 = (f32[129,512]{1,0:T(8,128)}, f32[129,512]{1,0:T(8,128)S(1)}, u32[]{:S(2)}, u32[]{:S(2)}) collective-permute-start(f32[129,512]{1,0:T(8,128)} %collective-permute-done), channel_id=1, source_target_pairs={{8,0},{16,8},{24,16},{32,24},{40,32},{48,40},{56,48},{64,56},{72,6... | collective-permute-start | bytes 792584 | tf_op jit(solution)/shard_map/ppermute | solution.py:20
  41.1 8.1 %collective-permute-start.8 = (f32[129,512]{1,0:T(8,128)}, f32[129,512]{1,0:T(8,128)S(1)}, u32[]{:S(2)}, u32[]{:S(2)}) collective-permute-start(f32[129,512]{1,0:T(8,128)} %collective-permute-done.7), channel_id=1, source_target_pairs={{0,8},{8,16},{16,24},{24,32},{32,40},{40,48},{48,56},{56,64},{64,7... | collective-permute-start | bytes 792584 | tf_op jit(solution)/shard_map/ppermute | solution.py:20
  46.5 8.4 %collective-permute-start.2 = (f32[129,512]{1,0:T(8,128)S(1)}, f32[129,512]{1,0:T(8,128)S(1)}, u32[]{:S(2)}, u32[]{:S(2)}) collective-permute-start(f32[129,512]{1,0:T(8,128)S(1)} %pad_maximum_fusion.2), channel_id=1, source_target_pairs={{16,0},{24,8},{32,16},{40,24},{48,32},{56,40},{64,48},{72,56},{80,... | collective-permute-start | bytes 792584 | tf_op jit(solution)/shard_map/ppermute | solution.py:20
  50.9 17.1 %collective-permute-start.9 = (f32[129,512]{1,0:T(8,128)S(1)}, f32[129,512]{1,0:T(8,128)S(1)}, u32[]{:S(2)}, u32[]{:S(2)}) collective-permute-start(f32[129,512]{1,0:T(8,128)S(1)} %pad_maximum_fusion.7), channel_id=1, source_target_pairs={{0,16},{8,24},{16,32},{24,40},{32,48},{40,56},{48,64},{56,72},{64,... | collective-permute-start | bytes 792584 | tf_op jit(solution)/shard_map/ppermute | solution.py:20
  55.1 15.4 %collective-permute-start.3 = (f32[129,512]{1,0:T(8,128)S(1)}, f32[129,512]{1,0:T(8,128)S(1)}, u32[]{:S(2)}, u32[]{:S(2)}) collective-permute-start(f32[129,512]{1,0:T(8,128)S(1)} %pad_maximum_fusion.3), channel_id=1, source_target_pairs={{32,0},{40,8},{48,16},{56,24},{64,32},{72,40},{80,48},{88,56},{96,... | collective-permute-start | bytes 792584 | tf_op jit(solution)/shard_map/ppermute | solution.py:20
  68.2 9.0 %collective-permute-start.10 = (f32[129,512]{1,0:T(8,128)S(1)}, f32[129,512]{1,0:T(8,128)S(1)}, u32[]{:S(2)}, u32[]{:S(2)}) collective-permute-start(f32[129,512]{1,0:T(8,128)S(1)} %pad_maximum_fusion.8), channel_id=1, source_target_pairs={{0,32},{8,40},{16,48},{24,56},{32,64},{40,72},{48,80},{56,88},{64,... | collective-permute-start | bytes 792584 | tf_op jit(solution)/shard_map/ppermute | solution.py:20
  70.6 14.6 %collective-permute-start.4 = (f32[129,512]{1,0:T(8,128)S(1)}, f32[129,512]{1,0:T(8,128)S(1)}, u32[]{:S(2)}, u32[]{:S(2)}) collective-permute-start(f32[129,512]{1,0:T(8,128)S(1)} %pad_maximum_fusion.4), channel_id=1, source_target_pairs={{64,0},{72,8},{80,16},{88,24},{96,32},{104,40},{112,48},{120,56},{... | collective-permute-start | bytes 792584 | tf_op jit(solution)/shard_map/ppermute | solution.py:20
  77.3 13.5 %collective-permute-start.11 = (f32[129,512]{1,0:T(8,128)S(1)}, f32[129,512]{1,0:T(8,128)S(1)}, u32[]{:S(2)}, u32[]{:S(2)}) collective-permute-start(f32[129,512]{1,0:T(8,128)S(1)} %pad_maximum_fusion.9), channel_id=1, source_target_pairs={{0,64},{8,72},{16,80},{24,88},{32,96},{40,104},{48,112},{56,120},{... | collective-permute-start | bytes 792584 | tf_op jit(solution)/shard_map/ppermute | solution.py:20
  85.3 16.6 %collective-permute-start.5 = (f32[129,512]{1,0:T(8,128)S(1)}, f32[129,512]{1,0:T(8,128)S(1)}, u32[]{:S(2)}, u32[]{:S(2)}) collective-permute-start(f32[129,512]{1,0:T(8,128)S(1)} %pad_maximum_fusion.5), channel_id=1, source_target_pairs={{128,0},{136,8},{144,16},{152,24},{160,32},{168,40},{176,48},{184,... | collective-permute-start | bytes 792584 | tf_op jit(solution)/shard_map/ppermute | solution.py:20
  90.9 12.5 %collective-permute-start.12 = (f32[129,512]{1,0:T(8,128)S(1)}, f32[129,512]{1,0:T(8,128)S(1)}, u32[]{:S(2)}, u32[]{:S(2)}) collective-permute-start(f32[129,512]{1,0:T(8,128)S(1)} %pad_maximum_fusion.10), channel_id=1, source_target_pairs={{0,128},{8,136},{16,144},{24,152},{32,160},{40,168},{48,176},{56,1... | collective-permute-start | bytes 792584 | tf_op jit(solution)/shard_map/ppermute | solution.py:20
  102.0 19.8 %collective-permute-start.6 = (f32[129,512]{1,0:T(8,128)S(1)}, f32[129,512]{1,0:T(8,128)S(1)}, u32[]{:S(2)}, u32[]{:S(2)}) collective-permute-start(f32[129,512]{1,0:T(8,128)S(1)} %pad_maximum_fusion.6), channel_id=1, source_target_pairs={{256,0},{264,8},{272,16},{280,24},{288,32},{296,40},{304,48},{312,... | collective-permute-start | bytes 792584 | tf_op jit(solution)/shard_map/ppermute | solution.py:20
  103.4 52.5 %collective-permute-start.13 = (f32[129,512]{1,0:T(8,128)S(1)}, f32[129,512]{1,0:T(8,128)S(1)}, u32[]{:S(2)}, u32[]{:S(2)}) collective-permute-start(f32[129,512]{1,0:T(8,128)S(1)} %pad_maximum_fusion.11), channel_id=1, source_target_pairs={{0,256},{8,264},{16,272},{24,280},{32,288},{40,296},{48,304},{56,3... | collective-permute-start | bytes 792584 | tf_op jit(solution)/shard_map/ppermute | solution.py:20
Sparse Core Ops, SparseCore 0:
  158.1 77.1 all-reduce.1
